TPU v7x, 32 devices: a whole 2x2x4 slice. The times are simulated.
32 devices in a mesh: layer: 8 (over z, x), row: 4 (over y, core).
Axes of the slice: x: 2, y: 2, z: 4, core: 2. Of those that a mesh axis runs over, the one named last changes fastest.
Arguments:
- right_side: float32 [8, 1024, 256], P('layer', 'row'), may hold values from -6 to 6
- reduce_factors: float32 [3, 8, 2, 1024, 1024], P(None, 'layer', None, 'row'), may hold values from -0.1875 to 0.1875
- solve_factors: float32 [8, 3, 1024, 1024], P('layer', None, 'row'), may hold values from -0.1875 to 0.1875
Outputs:
- solution: float32 [8, 1024, 256], P('layer', 'row')
All inputs are finite; a program needn't handle non-finite values.
Results may differ from a plain program's by a relative error of at most 0.00016.
Values sent between devices are 32-bit elements; how exact they have to be, the bound alone decides.
No kernel may reach another device: no remote copies, remote signals or barrier semaphores. Data moves between devices by JAX's collectives and lax.ppermute only.
A program may use at most 64 MiB of HBM per device.

v0:
```python
import jax
import jax.numpy as jnp
from jax import lax
from jax.sharding import PartitionSpec as P


def from_behind(shard, axis, by):
    devices = lax.axis_size(axis)
    pairs = [(i, i + by) for i in range(devices) if 0 <= i + by < devices]
    return lax.ppermute(shard, axis, pairs)


def product_of(left, right):
    return jnp.dot(left, right, precision=lax.Precision.HIGHEST, preferred_element_type=jnp.float32)


def neighbour_terms(vectors, left_mats, right_mats, stride):
    whole = lax.all_gather(vectors, "row", axis=1, tiled=True)
    lower = from_behind(whole, "layer", stride)
    upper = from_behind(whole, "layer", -stride)
    return (product_of(left_mats[0], lower[0]) + product_of(right_mats[0], upper[0]))[None]


def on_device(right_side, reduce_factors, solve_factors):
    layer_index = lax.axis_index("layer")
    level_count = reduce_factors.shape[0]
    current = right_side
    saved = right_side
    for level_index in range(level_count):
        stride = 1 << level_index
        terms = neighbour_terms(
            current, reduce_factors[level_index, :, 0], reduce_factors[level_index, :, 1], stride
        )
        saved = jnp.where(layer_index % (2 * stride) == stride, current, saved)
        current = jnp.where(layer_index % (2 * stride) == 0, current - terms, current)
    saved = jnp.where(layer_index == 0, current, saved)
    own_inverse = solve_factors[0, 0]
    base = product_of(own_inverse, lax.all_gather(saved, "row", axis=1, tiled=True)[0])[None]
    solution = jnp.where(layer_index == 0, base, jnp.zeros_like(base))
    for level_index in reversed(range(level_count)):
        stride = 1 << level_index
        terms = neighbour_terms(solution, solve_factors[:, 1], solve_factors[:, 2], stride)
        solution = jnp.where(layer_index % (2 * stride) == stride, base - terms, solution)
    return solution


def solution(mesh):
    placed = (
        P("layer", "row", None),
        P(None, "layer", None, "row", None),
        P("layer", None, "row", None),
    )
    return jax.shard_map(
        on_device, mesh=mesh, in_specs=placed, out_specs=P("layer", "row", None), check_vma=False
    )
```

profile of v0, /device:TPU:8, one launch (start us, length us, event | category | flops | bytes accessed | tf_op | source)
XLA Modules:
  0.0 427.2 jit_solution(3660228800837578581)
XLA Ops:
  6.5 0.0 all-gather.11.cloned.1.call-start
  6.5 0.7 all-gather.11.cloned.1.call-update
  7.3 0.0 all-gather.13.cloned.1.call-start
  7.3 19.5 %all-gather.11.cloned.1.call-done = f32[1,1024,256]{2,1,0:T(8,128)} async-done(((f32[1,256,256]{2,1,0:T(8,128)}), f32[1,1024,256]{2,1,0:T(8,128)}) %all-gather.11.cloned.1.call-update) | async-done | bytes 1048592 | tf_op jit(solution)/shard_map/all_gather | solution.py:18
  26.8 3.3 collective-permute-start.1
  30.2 2.5 collective-permute-start
  32.7 44.0 %collective-permute-done.1 = f32[1,1024,256]{2,1,0:T(8,128)S(1)} collective-permute-done((f32[1,1024,256]{2,1,0:T(8,128)}, f32[1,1024,256]{2,1,0:T(8,128)S(1)}, u32[]{:S(2)}, u32[]{:S(2)}) %collective-permute-start.1) | collective-permute-done | bytes 1048608 | tf_op jit(solution)/shard_map/ppermute | solution.py:10
  76.7 2.2 fusion.48
  78.9 0.0 collective-permute-done
  79.0 3.0 fusion.14
  82.0 0.0 all-gather.13.cloned.1.call-update
  82.0 0.0 all-gather.15.cloned.1.call-start
  82.0 15.9 %all-gather.13.cloned.1.call-done = f32[1,1024,256]{2,1,0:T(8,128)} async-done(((f32[1,256,256]{2,1,0:T(8,128)}), f32[1,1024,256]{2,1,0:T(8,128)}) %all-gather.13.cloned.1.call-update) | async-done | bytes 1048592 | tf_op jit(solution)/shard_map/all_gather | solution.py:18
  98.0 2.4 collective-permute-start.3
  100.4 3.4 collective-permute-start.2
  103.8 21.5 %collective-permute-done.3 = f32[1,1024,256]{2,1,0:T(8,128)S(1)} collective-permute-done((f32[1,1024,256]{2,1,0:T(8,128)}, f32[1,1024,256]{2,1,0:T(8,128)S(1)}, u32[]{:S(2)}, u32[]{:S(2)}) %collective-permute-start.3) | collective-permute-done | bytes 1048608 | tf_op jit(solution)/shard_map/ppermute | solution.py:10
  125.4 2.3 fusion.43
  127.6 0.0 copy-start.1
  127.7 0.0 collective-permute-done.2
  127.7 3.1 fusion.16
  130.7 0.0 copy-start
  130.7 0.0 all-gather.15.cloned.1.call-update
  130.8 0.0 all-gather.17.cloned.1.call-start
  130.8 16.7 %all-gather.15.cloned.1.call-done = f32[1,1024,256]{2,1,0:T(8,128)} async-done(((f32[1,256,256]{2,1,0:T(8,128)}), f32[1,1024,256]{2,1,0:T(8,128)}) %all-gather.15.cloned.1.call-update) | async-done | bytes 1048592 | tf_op jit(solution)/shard_map/all_gather | solution.py:18
  147.5 1.3 collective-permute-start.5
  148.8 7.4 %collective-permute-start.4 = (f32[1,1024,256]{2,1,0:T(8,128)}, f32[1,1024,256]{2,1,0:T(8,128)}, u32[]{:S(2)}, u32[]{:S(2)}) collective-permute-start(f32[1,1024,256]{2,1,0:T(8,128)} %all-gather.15.cloned.1.call-done), channel_id=1, source_target_pairs={{0,16},{4,20},{8,24},{12,28},{1,17},{5,21},{9,25},{13,29},{2,18},{... | collective-permute-start | bytes 3145736 | tf_op jit(solution)/shard_map/ppermute | solution.py:10
  156.2 19.8 %collective-permute-done.5 = f32[1,1024,256]{2,1,0:T(8,128)} collective-permute-done((f32[1,1024,256]{2,1,0:T(8,128)}, f32[1,1024,256]{2,1,0:T(8,128)}, u32[]{:S(2)}, u32[]{:S(2)}) %collective-permute-start.5) | collective-permute-done | bytes 1048608 | tf_op jit(solution)/shard_map/ppermute | solution.py:10
  176.0 2.6 fusion.38
  178.6 21.9 %collective-permute-done.4 = f32[1,1024,256]{2,1,0:T(8,128)} collective-permute-done((f32[1,1024,256]{2,1,0:T(8,128)}, f32[1,1024,256]{2,1,0:T(8,128)}, u32[]{:S(2)}, u32[]{:S(2)}) %collective-permute-start.4) | collective-permute-done | bytes 1048608 | tf_op jit(solution)/shard_map/ppermute | solution.py:10
  200.5 0.0 copy-done.1
  200.5 3.4 fusion.19
  203.9 0.0 all-gather.17.cloned.1.call-update
  203.9 0.0 all-gather.19.cloned.1.call-start
  204.0 17.9 %all-gather.17.cloned.1.call-done = f32[1,1024,256]{2,1,0:T(8,128)} async-done(((f32[1,256,256]{2,1,0:T(8,128)}), f32[1,1024,256]{2,1,0:T(8,128)}) %all-gather.17.cloned.1.call-update) | async-done | bytes 1048592 | tf_op jit(solution)/shard_map/all_gather | solution.py:38
  221.9 0.0 copy-done
  221.9 3.0 fusion.35
  224.9 0.7 select_bitcast_fusion
  225.6 0.0 all-gather.19.cloned.1.call-update
  225.7 0.0 all-gather.21.cloned.1.call-start
  225.7 16.8 %all-gather.19.cloned.1.call-done = f32[1024,256]{0,1:T(8,128)} async-done(((f32[256,256]{0,1:T(8,128)}), f32[1024,256]{0,1:T(8,128)}) %all-gather.19.cloned.1.call-update) | async-done | bytes 1048592 | tf_op jit(solution)/shard_map/all_gather | solution.py:18
  242.5 1.3 collective-permute-start.7
  243.8 5.6 %collective-permute-start.6 = (f32[1,1024,256]{1,2,0:T(8,128)}, f32[1,1024,256]{1,2,0:T(8,128)S(1)}, u32[]{:S(2)}, u32[]{:S(2)}) collective-permute-start(f32[1,1024,256]{1,2,0:T(8,128)} %bitcast.122), channel_id=1, source_target_pairs={{0,16},{4,20},{8,24},{12,28},{1,17},{5,21},{9,25},{13,29},{2,18},{... | collective-permute-start | bytes 3145736 | tf_op jit(solution)/shard_map/ppermute | solution.py:10
  249.4 21.5 %collective-permute-done.7 = f32[1,1024,256]{1,2,0:T(8,128)S(1)} collective-permute-done((f32[1,1024,256]{1,2,0:T(8,128)}, f32[1,1024,256]{1,2,0:T(8,128)S(1)}, u32[]{:S(2)}, u32[]{:S(2)}) %collective-permute-start.7) | collective-permute-done | bytes 1048608 | tf_op jit(solution)/shard_map/ppermute | solution.py:10
  270.9 1.0 fusion.28
  272.0 22.7 %collective-permute-done.6 = f32[1,1024,256]{1,2,0:T(8,128)S(1)} collective-permute-done((f32[1,1024,256]{1,2,0:T(8,128)}, f32[1,1024,256]{1,2,0:T(8,128)S(1)}, u32[]{:S(2)}, u32[]{:S(2)}) %collective-permute-start.6) | collective-permute-done | bytes 1048608 | tf_op jit(solution)/shard_map/ppermute | solution.py:10
  294.6 1.7 fusion.9
  296.4 0.0 all-gather.21.cloned.1.call-update
  296.4 0.2 all-gather.23.cloned.1.call-start
  296.6 17.5 %all-gather.21.cloned.1.call-done = f32[1024,256]{0,1:T(8,128)} async-done(((f32[256,256]{0,1:T(8,128)}), f32[1024,256]{0,1:T(8,128)}) %all-gather.21.cloned.1.call-update) | async-done | bytes 1048592 | tf_op jit(solution)/shard_map/all_gather | solution.py:18
  314.1 2.4 collective-permute-start.9
  316.6 3.4 collective-permute-start.8
  320.0 21.5 %collective-permute-done.9 = f32[1,1024,256]{1,2,0:T(8,128)S(1)} collective-permute-done((f32[1,1024,256]{1,2,0:T(8,128)}, f32[1,1024,256]{1,2,0:T(8,128)S(1)}, u32[]{:S(2)}, u32[]{:S(2)}) %collective-permute-start.9) | collective-permute-done | bytes 1048608 | tf_op jit(solution)/shard_map/ppermute | solution.py:10
  341.5 1.0 fusion.23
  342.6 1.1 collective-permute-done.8
  343.7 1.7 fusion.6
  345.5 0.0 all-gather.23.cloned.1.call-update
  345.5 17.9 %all-gather.23.cloned.1.call-done = f32[1024,256]{0,1:T(8,128)} async-done(((f32[256,256]{0,1:T(8,128)}), f32[1024,256]{0,1:T(8,128)}) %all-gather.23.cloned.1.call-update) | async-done | bytes 1048592 | tf_op jit(solution)/shard_map/all_gather | solution.py:18
  363.4 3.3 collective-permute-start.11
  366.7 2.5 collective-permute-start.10
  369.2 44.1 %collective-permute-done.11 = f32[1,1024,256]{1,2,0:T(8,128)} collective-permute-done((f32[1,1024,256]{1,2,0:T(8,128)}, f32[1,1024,256]{1,2,0:T(8,128)}, u32[]{:S(2)}, u32[]{:S(2)}) %collective-permute-start.11) | collective-permute-done | bytes 1048608 | tf_op jit(solution)/shard_map/ppermute | solution.py:10
  413.3 2.3 fusion.20
  415.6 0.0 collective-permute-done.10
  415.6 3.0 fusion.3
  418.6 1.8 copy.8
Async XLA Ops:
  6.5 20.3 %all-gather.11.cloned.1.call-start = ((), (), s32[]{:S(2)}) async-start(), calls=%async_computation | async-start | bytes 1310720 | tf_op jit(solution)/shard_map/all_gather | solution.py:18
  7.3 90.7 %all-gather.13.cloned.1.call-start = ((), (), s32[]{:S(2)}) async-start(), calls=%async_computation.1 | async-start | bytes 1310720 | tf_op jit(solution)/shard_map/all_gather | solution.py:18
  26.8 49.9 %collective-permute-start.1 = (f32[1,1024,256]{2,1,0:T(8,128)}, f32[1,1024,256]{2,1,0:T(8,128)S(1)}, u32[]{:S(2)}, u32[]{:S(2)}) collective-permute-start(f32[1,1024,256]{2,1,0:T(8,128)} %all-gather.11.cloned.1.call-done), channel_id=1, source_target_pairs={{4,0},{8,4},{12,8},{16,12},{20,16},{24,20},{28,24},{5,1},{9,5},{13... | collective-permute-start | bytes 3145736 | tf_op jit(solution)/shard_map/ppermute | solution.py:10
  30.2 48.8 %collective-permute-start = (f32[1,1024,256]{2,1,0:T(8,128)}, f32[1,1024,256]{2,1,0:T(8,128)S(1)}, u32[]{:S(2)}, u32[]{:S(2)}) collective-permute-start(f32[1,1024,256]{2,1,0:T(8,128)} %all-gather.11.cloned.1.call-done), channel_id=1, source_target_pairs={{0,4},{4,8},{8,12},{12,16},{16,20},{20,24},{24,28},{1,5},{5,9},{9,... | collective-permute-start | bytes 3145736 | tf_op jit(solution)/shard_map/ppermute | solution.py:10
  82.0 65.5 %all-gather.15.cloned.1.call-start = ((), (), s32[]{:S(2)}) async-start(), calls=%async_computation.2 | async-start | bytes 1310720 | tf_op jit(solution)/shard_map/all_gather | solution.py:18
  98.0 27.4 %collective-permute-start.3 = (f32[1,1024,256]{2,1,0:T(8,128)}, f32[1,1024,256]{2,1,0:T(8,128)S(1)}, u32[]{:S(2)}, u32[]{:S(2)}) collective-permute-start(f32[1,1024,256]{2,1,0:T(8,128)} %all-gather.13.cloned.1.call-done), channel_id=1, source_target_pairs={{8,0},{12,4},{16,8},{20,12},{24,16},{28,20},{9,1},{13,5},{17,9},{2... | collective-permute-start | bytes 3145736 | tf_op jit(solution)/shard_map/ppermute | solution.py:10
  100.4 27.3 %collective-permute-start.2 = (f32[1,1024,256]{2,1,0:T(8,128)}, f32[1,1024,256]{2,1,0:T(8,128)S(1)}, u32[]{:S(2)}, u32[]{:S(2)}) collective-permute-start(f32[1,1024,256]{2,1,0:T(8,128)} %all-gather.13.cloned.1.call-done), channel_id=1, source_target_pairs={{0,8},{4,12},{8,16},{12,20},{16,24},{20,28},{1,9},{5,13},{9,17},{1... | collective-permute-start | bytes 3145736 | tf_op jit(solution)/shard_map/ppermute | solution.py:10
  127.6 72.9 %copy-start.1 = (f32[1,256,256]{2,1,0:T(8,128)S(1)}, f32[1,256,256]{2,1,0:T(8,128)}, u32[]{:S(2)}) copy-start(f32[1,256,256]{2,1,0:T(8,128)} %fusion.14) | copy-start | bytes 786436
  130.7 91.1 %copy-start = (f32[1,3,256,1024]{3,2,1,0:T(8,128)S(1)}, f32[1,3,256,1024]{3,2,1,0:T(8,128)}, u32[]{:S(2)}) copy-start(f32[1,3,256,1024]{3,2,1,0:T(8,128)} %param.5) | copy-start | bytes 9437188
  130.8 91.1 %all-gather.17.cloned.1.call-start = ((), (), s32[]{:S(2)}) async-start(), calls=%async_computation.3 | async-start | bytes 1310720 | tf_op jit(solution)/shard_map/all_gather | solution.py:38
  147.5 28.5 %collective-permute-start.5 = (f32[1,1024,256]{2,1,0:T(8,128)}, f32[1,1024,256]{2,1,0:T(8,128)}, u32[]{:S(2)}, u32[]{:S(2)}) collective-permute-start(f32[1,1024,256]{2,1,0:T(8,128)} %all-gather.15.cloned.1.call-done), channel_id=1, source_target_pairs={{16,0},{20,4},{24,8},{28,12},{17,1},{21,5},{25,9},{29,13},{18,2},{... | collective-permute-start | bytes 3145736 | tf_op jit(solution)/shard_map/ppermute | solution.py:10
  148.8 51.7 %collective-permute-start.4 = (f32[1,1024,256]{2,1,0:T(8,128)}, f32[1,1024,256]{2,1,0:T(8,128)}, u32[]{:S(2)}, u32[]{:S(2)}) collective-permute-start(f32[1,1024,256]{2,1,0:T(8,128)} %all-gather.15.cloned.1.call-done), channel_id=1, source_target_pairs={{0,16},{4,20},{8,24},{12,28},{1,17},{5,21},{9,25},{13,29},{2,18},{... | collective-permute-start | bytes 3145736 | tf_op jit(solution)/shard_map/ppermute | solution.py:10
  203.9 38.6 %all-gather.19.cloned.1.call-start = ((), (), s32[]{:S(2)}) async-start(), calls=%async_computation.4 | async-start | bytes 1310720 | tf_op jit(solution)/shard_map/all_gather | solution.py:18
  225.7 88.5 %all-gather.21.cloned.1.call-start = ((), (), s32[]{:S(2)}) async-start(), calls=%async_computation.5 | async-start | bytes 1310720 | tf_op jit(solution)/shard_map/all_gather | solution.py:18
  242.5 28.4 %collective-permute-start.7 = (f32[1,1024,256]{1,2,0:T(8,128)}, f32[1,1024,256]{1,2,0:T(8,128)S(1)}, u32[]{:S(2)}, u32[]{:S(2)}) collective-permute-start(f32[1,1024,256]{1,2,0:T(8,128)} %bitcast.121), channel_id=1, source_target_pairs={{16,0},{20,4},{24,8},{28,12},{17,1},{21,5},{25,9},{29,13},{18,2},{... | collective-permute-start | bytes 3145736 | tf_op jit(solution)/shard_map/ppermute | solution.py:10
  243.8 50.8 %collective-permute-start.6 = (f32[1,1024,256]{1,2,0:T(8,128)}, f32[1,1024,256]{1,2,0:T(8,128)S(1)}, u32[]{:S(2)}, u32[]{:S(2)}) collective-permute-start(f32[1,1024,256]{1,2,0:T(8,128)} %bitcast.122), channel_id=1, source_target_pairs={{0,16},{4,20},{8,24},{12,28},{1,17},{5,21},{9,25},{13,29},{2,18},{... | collective-permute-start | bytes 3145736 | tf_op jit(solution)/shard_map/ppermute | solution.py:10
  296.4 67.0 %all-gather.23.cloned.1.call-start = ((), (), s32[]{:S(2)}) async-start(), calls=%async_computation.6 | async-start | bytes 1310720 | tf_op jit(solution)/shard_map/all_gather | solution.py:18
  314.1 27.4 %collective-permute-start.9 = (f32[1,1024,256]{1,2,0:T(8,128)}, f32[1,1024,256]{1,2,0:T(8,128)S(1)}, u32[]{:S(2)}, u32[]{:S(2)}) collective-permute-start(f32[1,1024,256]{1,2,0:T(8,128)} %bitcast.125), channel_id=1, source_target_pairs={{8,0},{12,4},{16,8},{20,12},{24,16},{28,20},{9,1},{13,5},{17,9},{2... | collective-permute-start | bytes 3145736 | tf_op jit(solution)/shard_map/ppermute | solution.py:10
  316.6 27.1 %collective-permute-start.8 = (f32[1,1024,256]{1,2,0:T(8,128)}, f32[1,1024,256]{1,2,0:T(8,128)S(1)}, u32[]{:S(2)}, u32[]{:S(2)}) collective-permute-start(f32[1,1024,256]{1,2,0:T(8,128)} %bitcast.126), channel_id=1, source_target_pairs={{0,8},{4,12},{8,16},{12,20},{16,24},{20,28},{1,9},{5,13},{9,17},{1... | collective-permute-start | bytes 3145736 | tf_op jit(solution)/shard_map/ppermute | solution.py:10
  363.4 50.0 %collective-permute-start.11 = (f32[1,1024,256]{1,2,0:T(8,128)}, f32[1,1024,256]{1,2,0:T(8,128)}, u32[]{:S(2)}, u32[]{:S(2)}) collective-permute-start(f32[1,1024,256]{1,2,0:T(8,128)} %bitcast.123), channel_id=1, source_target_pairs={{4,0},{8,4},{12,8},{16,12},{20,16},{24,20},{28,24},{5,1},{9,5},{13... | collective-permute-start | bytes 3145736 | tf_op jit(solution)/shard_map/ppermute | solution.py:10
  366.7 48.9 %collective-permute-start.10 = (f32[1,1024,256]{1,2,0:T(8,128)}, f32[1,1024,256]{1,2,0:T(8,128)}, u32[]{:S(2)}, u32[]{:S(2)}) collective-permute-start(f32[1,1024,256]{1,2,0:T(8,128)} %bitcast.124), channel_id=1, source_target_pairs={{0,4},{4,8},{8,12},{12,16},{16,20},{20,24},{24,28},{1,5},{5,9},{9,... | collective-permute-start | bytes 3145736 | tf_op jit(solution)/shard_map/ppermute | solution.py:10
Sparse Core Ops, SparseCore 0:
  8.9 17.8 all-gather.10
  82.1 15.8 all-gather.12
  130.9 16.5 all-gather.14
  204.0 17.7 all-gather.16
  225.8 16.7 all-gather.18
  296.5 17.5 all-gather.20
  345.6 17.7 all-gather.22
where the time goes:
time: 428 us; the launch traced here: 427 us
  waiting for transfers between devices  341 us (80%)
  starting transfers between devices  39.3 us (9%)
  matrix products  30.4 us (7%)
  between operations  13.7 us (3%)
    ppermute x12, waiting for transfers between devices, from_behind(): return lax.ppermute(shard, axis, pairs)  218 us
    all_gather x6, waiting for transfers between devices, neighbour_terms(): whole = lax.all_gather(vectors, 'row', axis=1, tiled=True)  104 us
    ppermute x12, starting transfers between devices, from_behind(): return lax.ppermute(shard, axis, pairs)  38.9 us
    dot_general x13, matrix products, product_of(): jnp.dot(left, right, precision=lax.Precision.HIGHEST, preferred_element_t...  30.4 us
    all_gather x1, waiting for transfers between devices, on_device(): lax.all_gather(saved, 'row', axis=1, tiled=True)[0]  17.9 us
  transfers between devices with their start and end apart: 19, of which 16 were waited for; matrix products, arithmetic and copies ran while one was open for 3% of the time, Pallas kernels for 0%

commit v1 on v0

--- a/solution.py
+++ b/solution.py
@@ -2,6 +2,13 @@
 import jax.numpy as jnp
 from jax import lax
 from jax.sharding import PartitionSpec as P
+
+
+def gather_over(block, axis, dim):
+    peers = lax.axis_size(axis)
+    blocks = jnp.stack([block for _ in range(peers)])
+    blocks = lax.all_to_all(blocks, axis, split_axis=0, concat_axis=0)
+    return jnp.concatenate(blocks, axis=dim)
 
 
 def from_behind(shard, axis, by):
@@ -35,7 +42,7 @@
         current = jnp.where(layer_index % (2 * stride) == 0, current - terms, current)
     saved = jnp.where(layer_index == 0, current, saved)
     own_inverse = solve_factors[0, 0]
-    base = product_of(own_inverse, lax.all_gather(saved, "row", axis=1, tiled=True)[0])[None]
+    base = product_of(own_inverse, gather_over(saved, "row", 1)[0])[None]
     solution = jnp.where(layer_index == 0, base, jnp.zeros_like(base))
     for level_index in reversed(range(level_count)):
         stride = 1 << level_index

time: 428 us -> 425 us (level)
  blocking collectives: 0 us -> 16.9 us
  waiting for transfers between devices: 341 us -> 325 us
    all_gather x1 -> x0, waiting for transfers between devices: 17.9 us -> none  [on_device(): lax.all_gather(saved, 'row', axis=1, tiled=True)[0]]
    all_to_all x0 -> x1, blocking collectives: none -> 16.9 us  [gather_over(): blocks = lax.all_to_all(blocks, axis, split_axis=0, concat_axis=0)]
  transfers between devices with their start and end apart: 19 -> 18, of which waited for: 16 -> 15; matrix products, arithmetic and copies ran while one was open for 3% -> 3% of each run, Pallas kernels for 0% -> 0%
where the time goes in v1:
time: 425 us; the launch traced here: 424 us
  waiting for transfers between devices  325 us (76%)
  starting transfers between devices  38.3 us (9%)
  matrix products  28.2 us (7%)
  blocking collectives  16.9 us (4%)
  between operations  13.7 us (3%)
    ppermute x12, waiting for transfers between devices, from_behind(): return lax.ppermute(shard, axis, pairs)  218 us
    all_gather x6, waiting for transfers between devices, neighbour_terms(): whole = lax.all_gather(vectors, 'row', axis=1, tiled=True)  106 us
    ppermute x12, starting transfers between devices, from_behind(): return lax.ppermute(shard, axis, pairs)  38.1 us
    dot_general x13, matrix products, product_of(): jnp.dot(left, right, precision=lax.Precision.HIGHEST, preferred_element_t...  28.2 us
    all_to_all x1, blocking collectives, gather_over(): blocks = lax.all_to_all(blocks, axis, split_axis=0, concat_axis=0)  16.9 us
  transfers between devices with their start and end apart: 18, of which 15 were waited for; matrix products, arithmetic and copies ran while one was open for 3% of the time, Pallas kernels for 0%

profile of v1, /device:TPU:8, one launch (start us, length us, event | category | flops | bytes accessed | tf_op | source)
XLA Modules:
  0.0 424.5 jit_solution(3235455694539176135)
XLA Ops:
  6.5 0.0 all-gather.10.cloned.1.call-start
  6.5 0.7 all-gather.10.cloned.1.call-update
  7.3 0.0 all-gather.12.cloned.1.call-start
  7.3 19.5 %all-gather.10.cloned.1.call-done = f32[1,1024,256]{2,1,0:T(8,128)} async-done(((f32[1,256,256]{2,1,0:T(8,128)}), f32[1,1024,256]{2,1,0:T(8,128)}) %all-gather.10.cloned.1.call-update) | async-done | bytes 1048592 | tf_op jit(solution)/shard_map/all_gather | solution.py:25
  26.8 3.3 collective-permute-start.1
  30.2 2.5 collective-permute-start
  32.7 44.0 %collective-permute-done.1 = f32[1,1024,256]{2,1,0:T(8,128)S(1)} collective-permute-done((f32[1,1024,256]{2,1,0:T(8,128)}, f32[1,1024,256]{2,1,0:T(8,128)S(1)}, u32[]{:S(2)}, u32[]{:S(2)}) %collective-permute-start.1) | collective-permute-done | bytes 1048608 | tf_op jit(solution)/shard_map/ppermute | solution.py:17
  76.7 2.2 fusion.48
  78.9 0.0 collective-permute-done
  79.0 3.0 fusion.14
  82.0 0.0 all-gather.12.cloned.1.call-update
  82.0 0.0 all-gather.14.cloned.1.call-start
  82.0 15.9 %all-gather.12.cloned.1.call-done = f32[1,1024,256]{2,1,0:T(8,128)} async-done(((f32[1,256,256]{2,1,0:T(8,128)}), f32[1,1024,256]{2,1,0:T(8,128)}) %all-gather.12.cloned.1.call-update) | async-done | bytes 1048592 | tf_op jit(solution)/shard_map/all_gather | solution.py:25
  98.0 2.4 collective-permute-start.3
  100.4 3.4 collective-permute-start.2
  103.8 21.5 %collective-permute-done.3 = f32[1,1024,256]{2,1,0:T(8,128)S(1)} collective-permute-done((f32[1,1024,256]{2,1,0:T(8,128)}, f32[1,1024,256]{2,1,0:T(8,128)S(1)}, u32[]{:S(2)}, u32[]{:S(2)}) %collective-permute-start.3) | collective-permute-done | bytes 1048608 | tf_op jit(solution)/shard_map/ppermute | solution.py:17
  125.4 2.3 fusion.43
  127.6 0.0 copy-start.1
  127.7 0.0 collective-permute-done.2
  127.7 3.1 fusion.16
  130.7 0.0 all-gather.14.cloned.1.call-update
  130.8 0.0 all-gather.16.cloned.1.call-start
  130.8 16.7 %all-gather.14.cloned.1.call-done = f32[1,1024,256]{2,1,0:T(8,128)} async-done(((f32[1,256,256]{2,1,0:T(8,128)}), f32[1,1024,256]{2,1,0:T(8,128)}) %all-gather.14.cloned.1.call-update) | async-done | bytes 1048592 | tf_op jit(solution)/shard_map/all_gather | solution.py:25
  147.5 1.3 collective-permute-start.5
  148.8 6.5 %collective-permute-start.4 = (f32[1,1024,256]{2,1,0:T(8,128)}, f32[1,1024,256]{2,1,0:T(8,128)}, u32[]{:S(2)}, u32[]{:S(2)}) collective-permute-start(f32[1,1024,256]{2,1,0:T(8,128)} %all-gather.14.cloned.1.call-done), channel_id=1, source_target_pairs={{0,16},{4,20},{8,24},{12,28},{1,17},{5,21},{9,25},{13,29},{2,18},{... | collective-permute-start | bytes 3145736 | tf_op jit(solution)/shard_map/ppermute | solution.py:17
  155.3 20.6 %collective-permute-done.5 = f32[1,1024,256]{2,1,0:T(8,128)S(1)} collective-permute-done((f32[1,1024,256]{2,1,0:T(8,128)}, f32[1,1024,256]{2,1,0:T(8,128)S(1)}, u32[]{:S(2)}, u32[]{:S(2)}) %collective-permute-start.5) | collective-permute-done | bytes 1048608 | tf_op jit(solution)/shard_map/ppermute | solution.py:17
  175.9 2.3 fusion.38
  178.2 0.0 copy-start
  178.2 21.4 %collective-permute-done.4 = f32[1,1024,256]{2,1,0:T(8,128)} collective-permute-done((f32[1,1024,256]{2,1,0:T(8,128)}, f32[1,1024,256]{2,1,0:T(8,128)}, u32[]{:S(2)}, u32[]{:S(2)}) %collective-permute-start.4) | collective-permute-done | bytes 1048608 | tf_op jit(solution)/shard_map/ppermute | solution.py:17
  199.6 0.0 copy-done.1
  199.6 2.7 fusion.20
  202.3 0.1 stack.2
  202.4 16.9 %all_to_all.5 = f32[4,1,256,256]{3,2,1,0:T(8,128)S(1)} all-to-all(f32[4,1,256,256]{3,2,1,0:T(8,128)S(1)} %stack.2), channel_id=1, replica_groups=mesh['layer'=8,'row'=4] {'row'}, dimensions={0} | all-to-all | bytes 2097152 | tf_op jit(solution)/shard_map/all_to_all | solution.py:10
  219.3 0.0 copy-done
  219.3 1.8 fusion.36
  221.1 0.7 select_bitcast_fusion
  221.8 0.0 all-gather.16.cloned.1.call-update
  221.8 0.0 all-gather.18.cloned.1.call-start
  221.9 17.9 %all-gather.16.cloned.1.call-done = f32[1024,256]{0,1:T(8,128)} async-done(((f32[256,256]{0,1:T(8,128)}), f32[1024,256]{0,1:T(8,128)}) %all-gather.16.cloned.1.call-update) | async-done | bytes 1048592 | tf_op jit(solution)/shard_map/all_gather | solution.py:25
  239.8 1.3 collective-permute-start.7
  241.0 5.8 %collective-permute-start.6 = (f32[1,1024,256]{1,2,0:T(8,128)}, f32[1,1024,256]{1,2,0:T(8,128)S(1)}, u32[]{:S(2)}, u32[]{:S(2)}) collective-permute-start(f32[1,1024,256]{1,2,0:T(8,128)} %bitcast.126), channel_id=1, source_target_pairs={{0,16},{4,20},{8,24},{12,28},{1,17},{5,21},{9,25},{13,29},{2,18},{... | collective-permute-start | bytes 3145736 | tf_op jit(solution)/shard_map/ppermute | solution.py:17
  246.8 21.3 %collective-permute-done.7 = f32[1,1024,256]{1,2,0:T(8,128)S(1)} collective-permute-done((f32[1,1024,256]{1,2,0:T(8,128)}, f32[1,1024,256]{1,2,0:T(8,128)S(1)}, u32[]{:S(2)}, u32[]{:S(2)}) %collective-permute-start.7) | collective-permute-done | bytes 1048608 | tf_op jit(solution)/shard_map/ppermute | solution.py:17
  268.1 1.0 fusion.29
  269.2 22.7 %collective-permute-done.6 = f32[1,1024,256]{1,2,0:T(8,128)S(1)} collective-permute-done((f32[1,1024,256]{1,2,0:T(8,128)}, f32[1,1024,256]{1,2,0:T(8,128)S(1)}, u32[]{:S(2)}, u32[]{:S(2)}) %collective-permute-start.6) | collective-permute-done | bytes 1048608 | tf_op jit(solution)/shard_map/ppermute | solution.py:17
  291.8 1.7 fusion.9
  293.6 0.0 all-gather.18.cloned.1.call-update
  293.6 0.0 all-gather.20.cloned.1.call-start
  293.7 17.7 %all-gather.18.cloned.1.call-done = f32[1024,256]{0,1:T(8,128)} async-done(((f32[256,256]{0,1:T(8,128)}), f32[1024,256]{0,1:T(8,128)}) %all-gather.18.cloned.1.call-update) | async-done | bytes 1048592 | tf_op jit(solution)/shard_map/all_gather | solution.py:25
  311.4 2.4 collective-permute-start.9
  313.8 3.4 collective-permute-start.8
  317.2 21.5 %collective-permute-done.9 = f32[1,1024,256]{1,2,0:T(8,128)S(1)} collective-permute-done((f32[1,1024,256]{1,2,0:T(8,128)}, f32[1,1024,256]{1,2,0:T(8,128)S(1)}, u32[]{:S(2)}, u32[]{:S(2)}) %collective-permute-start.9) | collective-permute-done | bytes 1048608 | tf_op jit(solution)/shard_map/ppermute | solution.py:17
  338.8 1.0 fusion.24
  339.8 1.1 collective-permute-done.8
  340.9 1.8 fusion.6
  342.7 0.0 all-gather.20.cloned.1.call-update
  342.7 17.9 %all-gather.20.cloned.1.call-done = f32[1024,256]{0,1:T(8,128)} async-done(((f32[256,256]{0,1:T(8,128)}), f32[1024,256]{0,1:T(8,128)}) %all-gather.20.cloned.1.call-update) | async-done | bytes 1048592 | tf_op jit(solution)/shard_map/all_gather | solution.py:25
  360.6 3.3 collective-permute-start.11
  363.9 2.5 collective-permute-start.10
  366.4 44.1 %collective-permute-done.11 = f32[1,1024,256]{1,2,0:T(8,128)} collective-permute-done((f32[1,1024,256]{1,2,0:T(8,128)}, f32[1,1024,256]{1,2,0:T(8,128)}, u32[]{:S(2)}, u32[]{:S(2)}) %collective-permute-start.11) | collective-permute-done | bytes 1048608 | tf_op jit(solution)/shard_map/ppermute | solution.py:17
  410.6 2.3 fusion.21
  412.8 0.0 collective-permute-done.10
  412.8 3.0 fusion.3
  415.8 1.8 copy.8
Async XLA Ops:
  6.5 20.3 %all-gather.10.cloned.1.call-start = ((), (), s32[]{:S(2)}) async-start(), calls=%async_computation.1 | async-start | bytes 1310720 | tf_op jit(solution)/shard_map/all_gather | solution.py:25
  7.3 90.7 %all-gather.12.cloned.1.call-start = ((), (), s32[]{:S(2)}) async-start(), calls=%async_computation.2 | async-start | bytes 1310720 | tf_op jit(solution)/shard_map/all_gather | solution.py:25
  26.8 49.9 %collective-permute-start.1 = (f32[1,1024,256]{2,1,0:T(8,128)}, f32[1,1024,256]{2,1,0:T(8,128)S(1)}, u32[]{:S(2)}, u32[]{:S(2)}) collective-permute-start(f32[1,1024,256]{2,1,0:T(8,128)} %all-gather.10.cloned.1.call-done), channel_id=1, source_target_pairs={{4,0},{8,4},{12,8},{16,12},{20,16},{24,20},{28,24},{5,1},{9,5},{13... | collective-permute-start | bytes 3145736 | tf_op jit(solution)/shard_map/ppermute | solution.py:17
  30.2 48.8 %collective-permute-start = (f32[1,1024,256]{2,1,0:T(8,128)}, f32[1,1024,256]{2,1,0:T(8,128)S(1)}, u32[]{:S(2)}, u32[]{:S(2)}) collective-permute-start(f32[1,1024,256]{2,1,0:T(8,128)} %all-gather.10.cloned.1.call-done), channel_id=1, source_target_pairs={{0,4},{4,8},{8,12},{12,16},{16,20},{20,24},{24,28},{1,5},{5,9},{9,... | collective-permute-start | bytes 3145736 | tf_op jit(solution)/shard_map/ppermute | solution.py:17
  82.0 65.5 %all-gather.14.cloned.1.call-start = ((), (), s32[]{:S(2)}) async-start(), calls=%async_computation.3 | async-start | bytes 1310720 | tf_op jit(solution)/shard_map/all_gather | solution.py:25
  98.0 27.4 %collective-permute-start.3 = (f32[1,1024,256]{2,1,0:T(8,128)}, f32[1,1024,256]{2,1,0:T(8,128)S(1)}, u32[]{:S(2)}, u32[]{:S(2)}) collective-permute-start(f32[1,1024,256]{2,1,0:T(8,128)} %all-gather.12.cloned.1.call-done), channel_id=1, source_target_pairs={{8,0},{12,4},{16,8},{20,12},{24,16},{28,20},{9,1},{13,5},{17,9},{2... | collective-permute-start | bytes 3145736 | tf_op jit(solution)/shard_map/ppermute | solution.py:17
  100.4 27.3 %collective-permute-start.2 = (f32[1,1024,256]{2,1,0:T(8,128)}, f32[1,1024,256]{2,1,0:T(8,128)S(1)}, u32[]{:S(2)}, u32[]{:S(2)}) collective-permute-start(f32[1,1024,256]{2,1,0:T(8,128)} %all-gather.12.cloned.1.call-done), channel_id=1, source_target_pairs={{0,8},{4,12},{8,16},{12,20},{16,24},{20,28},{1,9},{5,13},{9,17},{1... | collective-permute-start | bytes 3145736 | tf_op jit(solution)/shard_map/ppermute | solution.py:17
  127.6 72.0 %copy-start.1 = (f32[1,256,256]{2,1,0:T(8,128)S(1)}, f32[1,256,256]{2,1,0:T(8,128)}, u32[]{:S(2)}) copy-start(f32[1,256,256]{2,1,0:T(8,128)} %fusion.14) | copy-start | bytes 786436
  130.8 109.0 %all-gather.16.cloned.1.call-start = ((), (), s32[]{:S(2)}) async-start(), calls=%async_computation.4 | async-start | bytes 1310720 | tf_op jit(solution)/shard_map/all_gather | solution.py:25
  147.5 28.4 %collective-permute-start.5 = (f32[1,1024,256]{2,1,0:T(8,128)}, f32[1,1024,256]{2,1,0:T(8,128)S(1)}, u32[]{:S(2)}, u32[]{:S(2)}) collective-permute-start(f32[1,1024,256]{2,1,0:T(8,128)} %all-gather.14.cloned.1.call-done), channel_id=1, source_target_pairs={{16,0},{20,4},{24,8},{28,12},{17,1},{21,5},{25,9},{29,13},{18,2},{... | collective-permute-start | bytes 3145736 | tf_op jit(solution)/shard_map/ppermute | solution.py:17
  148.8 50.8 %collective-permute-start.4 = (f32[1,1024,256]{2,1,0:T(8,128)}, f32[1,1024,256]{2,1,0:T(8,128)}, u32[]{:S(2)}, u32[]{:S(2)}) collective-permute-start(f32[1,1024,256]{2,1,0:T(8,128)} %all-gather.14.cloned.1.call-done), channel_id=1, source_target_pairs={{0,16},{4,20},{8,24},{12,28},{1,17},{5,21},{9,25},{13,29},{2,18},{... | collective-permute-start | bytes 3145736 | tf_op jit(solution)/shard_map/ppermute | solution.py:17
  178.2 41.0 %copy-start = (f32[1,3,256,1024]{3,2,1,0:T(8,128)S(1)}, f32[1,3,256,1024]{3,2,1,0:T(8,128)}, u32[]{:S(2)}) copy-start(f32[1,3,256,1024]{3,2,1,0:T(8,128)} %param.5) | copy-start | bytes 9437188
  221.8 89.5 %all-gather.18.cloned.1.call-start = ((), (), s32[]{:S(2)}) async-start(), calls=%async_computation.5 | async-start | bytes 1310720 | tf_op jit(solution)/shard_map/all_gather | solution.py:25
  239.8 28.4 %collective-permute-start.7 = (f32[1,1024,256]{1,2,0:T(8,128)}, f32[1,1024,256]{1,2,0:T(8,128)S(1)}, u32[]{:S(2)}, u32[]{:S(2)}) collective-permute-start(f32[1,1024,256]{1,2,0:T(8,128)} %bitcast.125), channel_id=1, source_target_pairs={{16,0},{20,4},{24,8},{28,12},{17,1},{21,5},{25,9},{29,13},{18,2},{... | collective-permute-start | bytes 3145736 | tf_op jit(solution)/shard_map/ppermute | solution.py:17
  241.0 50.8 %collective-permute-start.6 = (f32[1,1024,256]{1,2,0:T(8,128)}, f32[1,1024,256]{1,2,0:T(8,128)S(1)}, u32[]{:S(2)}, u32[]{:S(2)}) collective-permute-start(f32[1,1024,256]{1,2,0:T(8,128)} %bitcast.126), channel_id=1, source_target_pairs={{0,16},{4,20},{8,24},{12,28},{1,17},{5,21},{9,25},{13,29},{2,18},{... | collective-permute-start | bytes 3145736 | tf_op jit(solution)/shard_map/ppermute | solution.py:17
  293.6 67.0 %all-gather.20.cloned.1.call-start = ((), (), s32[]{:S(2)}) async-start(), calls=%async_computation.6 | async-start | bytes 1310720 | tf_op jit(solution)/shard_map/all_gather | solution.py:25
  311.4 27.4 %collective-permute-start.9 = (f32[1,1024,256]{1,2,0:T(8,128)}, f32[1,1024,256]{1,2,0:T(8,128)S(1)}, u32[]{:S(2)}, u32[]{:S(2)}) collective-permute-start(f32[1,1024,256]{1,2,0:T(8,128)} %bitcast.129), channel_id=1, source_target_pairs={{8,0},{12,4},{16,8},{20,12},{24,16},{28,20},{9,1},{13,5},{17,9},{2... | collective-permute-start | bytes 3145736 | tf_op jit(solution)/shard_map/ppermute | solution.py:17
  313.8 27.1 %collective-permute-start.8 = (f32[1,1024,256]{1,2,0:T(8,128)}, f32[1,1024,256]{1,2,0:T(8,128)S(1)}, u32[]{:S(2)}, u32[]{:S(2)}) collective-permute-start(f32[1,1024,256]{1,2,0:T(8,128)} %bitcast.130), channel_id=1, source_target_pairs={{0,8},{4,12},{8,16},{12,20},{16,24},{20,28},{1,9},{5,13},{9,17},{1... | collective-permute-start | bytes 3145736 | tf_op jit(solution)/shard_map/ppermute | solution.py:17
  360.6 50.0 %collective-permute-start.11 = (f32[1,1024,256]{1,2,0:T(8,128)}, f32[1,1024,256]{1,2,0:T(8,128)}, u32[]{:S(2)}, u32[]{:S(2)}) collective-permute-start(f32[1,1024,256]{1,2,0:T(8,128)} %bitcast.127), channel_id=1, source_target_pairs={{4,0},{8,4},{12,8},{16,12},{20,16},{24,20},{28,24},{5,1},{9,5},{13... | collective-permute-start | bytes 3145736 | tf_op jit(solution)/shard_map/ppermute | solution.py:17
  363.9 48.9 %collective-permute-start.10 = (f32[1,1024,256]{1,2,0:T(8,128)}, f32[1,1024,256]{1,2,0:T(8,128)}, u32[]{:S(2)}, u32[]{:S(2)}) collective-permute-start(f32[1,1024,256]{1,2,0:T(8,128)} %bitcast.128), channel_id=1, source_target_pairs={{0,4},{4,8},{8,12},{12,16},{16,20},{20,24},{24,28},{1,5},{5,9},{9,... | collective-permute-start | bytes 3145736 | tf_op jit(solution)/shard_map/ppermute | solution.py:17
Sparse Core Ops, SparseCore 0:
  8.9 17.8 all-gather.9
  82.1 15.8 all-gather.11
  130.9 16.5 all-gather.13
  221.9 17.7 all-gather.15
  293.7 17.5 all-gather.17
  342.8 17.7 all-gather.19
